TPU v7x, 128 devices: a whole 4x4x4 slice. The times are simulated.
128 devices in a mesh: lat: 16 (over x, y), var: 8 (over z, core).
Axes of the slice: x: 4, y: 4, z: 4, core: 2. Of those that a mesh axis runs over, the one named last changes fastest.
Arguments:
- patches: bfloat16 [96, 192, 1024], P('lat', 'var'), may hold values from -6 to 6
- norm_gain: float32 [1024], replicated, may hold values from 0.25 to 1.75
- input_proj: bfloat16 [1024, 3072], replicated, may hold values from -7 to 7
- output_proj: bfloat16 [1024, 1024], replicated, may hold values from -0.1875 to 0.1875
- level_scale: float32 [40, 1024], P('var'), may hold values from 0.1 to 1.9
- level_shift: float32 [40, 1024], P('var'), may hold values from -3 to 3
- head_weight: bfloat16 [40, 1024, 320], P('var', 'lat'), may hold values from -0.1875 to 0.1875
- targets: bfloat16 [40, 96, 192, 320], P('var', 'lat'), may hold values from -6 to 6
- level_counts: int32 [4], replicated, may hold values from 13 to 37
- tile_dataset: int32 [16, 8], P('lat'), may hold values from 0 to 3
- slot_level: int32 [40], P('var'), may hold values from 0 to 39, as said below
Outputs:
- latent: bfloat16 [96, 192, 1024], P('lat', 'var')
- grad_latent: bfloat16 [96, 192, 1024], P('lat', 'var')
- grad_head: float32 [40, 1024, 320], P('var', 'lat')
Inputs may be any that keep to these rules, and one draw needn't show every extreme that they name: `slot_level`: for each j, slots j * 5 to (j + 1) * 5 - 1 hold the levels j * 5 to (j + 1) * 5 - 1 in some order.
All inputs are finite; a program needn't handle non-finite values.
Results may differ from a plain program's by a relative error of at most 0.012.
Values may be sent and summed in bfloat16 or wider, within the bound.
A program may use at most 128 MiB of HBM per device.

v0:
```python
import math
import jax
import jax.numpy as jnp
from jax import lax
from jax.sharding import PartitionSpec as P

HEADS = 16
WH = 6
WW = 12
EPS = 1e-05


def padded(array, sides, width, wrap):
    for axis, dim in sides:
        size, length = (lax.axis_size(axis), array.shape[dim])
        up = [(i, (i + 1) % size) for i in range(size if wrap else size - 1)]
        down = [(j, i) for i, j in up]
        last = lax.slice_in_dim(array, length - width, length, axis=dim)
        initial = lax.slice_in_dim(array, 0, width, axis=dim)
        before = lax.ppermute(last, axis, up)
        after = lax.ppermute(initial, axis, down)
        array = jnp.concatenate([before, array, after], axis=dim)
    return array


def layer_norm(values, gain):
    wide = values.astype(jnp.float32)
    average = jnp.mean(wide, axis=-1, keepdims=True)
    centred = wide - average
    variance = jnp.mean(centred * centred, axis=-1, keepdims=True)
    return (centred * lax.rsqrt(variance + EPS) * gain).astype(jnp.bfloat16)


def window_attention(query_ext, keyval, row_valid, heads):
    ext_rows, ext_cols, width = query_ext.shape
    head_size = width // heads
    win_rows = ext_rows // WH
    win_cols = ext_cols // WW

    def split(values, parts):
        shaped = values.reshape(win_rows, WH, win_cols, WW, parts, heads, head_size)
        return shaped.transpose(0, 2, 1, 3, 4, 5, 6).reshape(
            win_rows * win_cols, WH * WW, parts, heads, head_size
        )

    query_win = split(query_ext, 1)[:, :, 0]
    pairs = split(keyval, 2)
    key_win = pairs[:, :, 0]
    value_win = pairs[:, :, 1]
    key_mask = jnp.broadcast_to(
        row_valid.reshape(win_rows, 1, WH, 1), (win_rows, win_cols, WH, WW)
    ).reshape(win_rows * win_cols, WH * WW)
    scores = jnp.einsum(
        "wqhd,wkhd->whqk", query_win, key_win, preferred_element_type=jnp.float32
    ) / math.sqrt(head_size)
    scores = jnp.where(key_mask[:, None, None, :], scores, -jnp.inf)
    peak = jnp.max(scores, axis=-1, keepdims=True)
    weights = jnp.exp(scores - peak)
    probs = (weights / jnp.sum(weights, axis=-1, keepdims=True)).astype(jnp.bfloat16)
    mixed = jnp.einsum("whqk,wkhd->wqhd", probs, value_win, preferred_element_type=jnp.float32)
    return (
        mixed.reshape(win_rows, win_cols, WH, WW, width)
        .transpose(0, 2, 1, 3, 4)
        .reshape(ext_rows, ext_cols, width)
    )


def slot_terms(piece, target_rows, live_cols, level_scale, level_shift, heads_full):
    piece_wide = piece.astype(jnp.float32)
    rows = (
        piece_wide[None] * level_scale[:, None, None, :] + level_shift[:, None, None, :]
    ).astype(jnp.bfloat16)
    predicted = jnp.einsum("krnd,kdo->krno", rows, heads_full, preferred_element_type=jnp.float32)
    errors = ((predicted - target_rows.astype(jnp.float32)) * live_cols[:, None, :, None]).astype(
        jnp.bfloat16
    )
    back_grad = jnp.einsum("krno,kdo->krnd", errors, heads_full, preferred_element_type=jnp.float32)
    piece_grad = jnp.sum(back_grad * level_scale[:, None, None, :], axis=0)
    head_add = jnp.einsum("krnd,krno->dko", rows, errors, preferred_element_type=jnp.float32)
    return (piece_grad, head_add)


def local(
    patches,
    norm_gain,
    input_proj,
    output_proj,
    level_scale,
    level_shift,
    head_weight,
    targets,
    level_counts,
    tile_dataset,
    slot_level,
):
    band_rows, band_cols, width = patches.shape
    half_rows = WH // 2
    half_cols = WW // 2
    lat_count = lax.axis_size("lat")
    var_count = lax.axis_size("var")
    lat_place = lax.axis_index("lat")
    ext_rows = band_rows + WH
    ext_cols = band_cols + WW
    extended = padded(patches, (("lat", 0),), half_rows, False)
    extended = padded(extended, (("var", 1),), half_cols, True)
    normed_ext = layer_norm(extended, norm_gain)
    keyval = jnp.dot(
        normed_ext.reshape(-1, width), input_proj[:, width:], preferred_element_type=jnp.float32
    )
    keyval = keyval.astype(jnp.bfloat16).reshape(ext_rows, ext_cols, 2 * width)
    normed = normed_ext[half_rows : half_rows + band_rows, half_cols : half_cols + band_cols]
    queries = jnp.dot(
        normed.reshape(-1, width), input_proj[:, :width], preferred_element_type=jnp.float32
    )
    queries = queries.astype(jnp.bfloat16).reshape(band_rows, band_cols, width)
    query_ext = jnp.pad(queries, ((half_rows, WH - half_rows), (half_cols, WW - half_cols), (0, 0)))
    global_row = lat_place * band_rows - half_rows + jnp.arange(ext_rows, dtype=jnp.int32)
    row_valid = (global_row >= 0) & (global_row < lat_count * band_rows)
    mixed = window_attention(query_ext, keyval, row_valid, HEADS)
    attn = mixed[half_rows : half_rows + band_rows, half_cols : half_cols + band_cols].astype(
        jnp.bfloat16
    )
    update = jnp.dot(
        attn.reshape(-1, width), output_proj, preferred_element_type=jnp.float32
    ).reshape(band_rows, band_cols, width)
    latent = (patches.astype(jnp.float32) + update).astype(jnp.bfloat16)
    dataset_row = tile_dataset[0]
    dataset_ids = jnp.arange(level_counts.shape[0], dtype=jnp.int32)
    tile_levels = jnp.sum(
        jnp.where(dataset_row[:, None] == dataset_ids[None, :], level_counts[None, :], 0), axis=1
    )
    live_tiles = (slot_level[None, :] < tile_levels[:, None]).astype(jnp.float32)
    heads_full = lax.all_gather(head_weight, "lat", axis=1, tiled=True)
    tile_ids = jnp.arange(var_count, dtype=jnp.int32)
    piece = lax.all_gather(latent, "var", axis=1, tiled=True)
    piece_cols = piece.shape[1]
    column_tile = jnp.arange(piece_cols, dtype=jnp.int32) // band_cols
    onehot = (column_tile[:, None] == tile_ids[None, :]).astype(jnp.float32)
    column_live = jnp.dot(onehot, live_tiles)
    piece_grad, head_add = slot_terms(
        piece, targets, column_live.T, level_scale, level_shift, heads_full
    )
    latent_terms = piece_grad
    latent_terms, head_terms = (latent_terms, head_add)
    grad_latent = lax.psum_scatter(
        latent_terms.astype(jnp.bfloat16), "var", scatter_dimension=1, tiled=True
    )
    head_terms = head_terms * (1.0 / math.sqrt(lat_count * band_rows * var_count * band_cols))
    share_rows = width // lat_count
    mine = lax.psum_scatter(
        head_terms.astype(jnp.bfloat16), "lat", scatter_dimension=0, tiled=True
    ).astype(jnp.float32)
    grad_head = jnp.transpose(mine, (1, 0, 2))
    return (latent, grad_latent, grad_head)


def solution(mesh):
    in_specs = (
        P("lat", "var", None),
        P(),
        P(),
        P(),
        P("var", None),
        P("var", None),
        P("var", "lat", None),
        P("var", "lat", None, None),
        P(),
        P("lat", None),
        P("var"),
    )
    out_specs = (P("lat", "var", None), P("lat", "var", None), P("var", "lat", None))
    return jax.shard_map(local, mesh=mesh, in_specs=in_specs, out_specs=out_specs, check_vma=False)
```

profile of v0, /device:TPU:0, one launch (start us, length us, event | category | flops | bytes accessed | tf_op | source)
XLA Modules:
  0.0 313.8 jit_solution(12802649083848093492)
XLA Ops:
  8.4 3.6 %collective-permute-start = (bf16[3,24,1024]{2,1,0:T(8,128)(2,1)S(1)}, bf16[3,24,1024]{2,1,0:T(8,128)(2,1)S(1)}, u32[]{:S(2)}, u32[]{:S(2)}) collective-permute-start(bf16[3,24,1024]{2,1,0:T(8,128)(2,1)S(1)} %get-tuple-element.25), channel_id=1, source_target_pairs={{0,8},{8,16},{16,24},{24,32},{32,40},{40,48},{48,56},{56,64},{64,7... | collective-permute-start | bytes 442376 | tf_op jit(solution)/shard_map/ppermute | solution.py:20
  16.0 3.1 collective-permute-done.1
  19.3 2.9 collective-permute-start.3
  22.4 3.2 %collective-permute-done.2 = bf16[12,6,1024]{2,1,0:T(8,128)(2,1)S(1)} collective-permute-done((bf16[12,6,1024]{2,1,0:T(8,128)(2,1)S(1)}, bf16[12,6,1024]{2,1,0:T(8,128)(2,1)S(1)}, u32[]{:S(2)}, u32[]{:S(2)}) %collective-permute-start.2) | collective-permute-done | bytes 147488 | tf_op jit(solution)/shard_map/ppermute | solution.py:20
  29.7 2.7 reshape.102
  38.0 3.2 %copy.48 = bf16[2,3,6,12,1,16,64]{6,5,3,2,1,0,4:T(8,128)(2,1)} copy(bf16[2,3,6,12,1,16,64]{6,5,3,1,2,0,4:T(8,128)(2,1)} %bitcast.58) | data formatting | bytes 1769472 | tf_op jit(solution)/shard_map/transpose | solution.py:42
  41.2 5.5 %fusion.15 = bf16[432,2048]{1,0:T(8,128)(2,1)} fusion(bf16[1024,3072]{1,0:T(8,128)(2,1)} %param.13, f32[432,1024]{1,0:T(8,128)S(1)} %copy-done.2, f32[1024]{0:T(1024)S(1)} %copy-done.4, f32[432]{0:T(512)S(1)} %rsqrt.13, f32[432]{0:T(512)S(1)} %div.33), kind=kOutput, calls=%fused_computation.22 | convolution fusion | flops 1814593536 | bytes 7740800 | tf_op jit(solution)/shard_map/dot_general | solution.py:107
  46.8 6.4 %reshape_reshape.3 = bf16[2,6,3,12,2,16,64]{6,5,4,3,2,1,0:T(8,128)(2,1)} reshape(bf16[432,2048]{1,0:T(8,128)(2,1)} %fusion.15) | data formatting | bytes 3538944 | tf_op jit(solution)/shard_map/reshape;reshape | solution.py:41
  53.1 2.6 copy.46
  55.7 2.6 fusion.59
  58.3 4.0 %copy.61 = bf16[6,72,1,16,64]{1,4,3,0,2:T(8,128)(2,1)} copy(bf16[6,72,1,16,64]{4,3,2,1,0:T(8,128)(2,1)} %get-tuple-element.18) | data formatting | bytes 1769472
  62.4 4.0 %copy.62 = bf16[6,72,1,16,64]{1,4,3,0,2:T(8,128)(2,1)} copy(bf16[6,72,1,16,64]{4,3,2,1,0:T(8,128)(2,1)} %get-tuple-element.19) | data formatting | bytes 1769472
  66.4 3.1 fusion.25
  73.2 4.0 %copy.52 = bf16[6,72,16,64]{3,2,1,0:T(8,128)(2,1)} copy(bf16[6,72,16,64]{1,3,2,0:T(8,128)(2,1)} %fusion.34) | data formatting | bytes 1769472 | tf_op jit(solution)/shard_map/whqk,wkhd->wqhd/transpose | solution.py:60
  77.2 3.9 %reshape.100 = bf16[2,3,6,12,1024]{4,3,2,1,0:T(8,128)(2,1)} reshape(bf16[6,72,16,64]{3,2,1,0:T(8,128)(2,1)} %copy.52) | data formatting | bytes 1769472 | tf_op jit(solution)/shard_map/reshape | solution.py:62
  87.1 28.5 %all-gather.3.cloned.1.call-done = bf16[6,192,1024]{2,1,0:T(8,128)(2,1)} async-done(((bf16[6,24,1024]{2,1,0:T(8,128)(2,1)}), bf16[6,192,1024]{2,1,0:T(8,128)(2,1)}) %all-gather.3.cloned.1.call-update) | async-done | bytes 2359312 | tf_op jit(solution)/shard_map/all_gather | solution.py:135
  115.6 4.3 %convert_element_type.67 = f32[6,192,1024]{2,1,0:T(8,128)} convert(bf16[6,192,1024]{2,1,0:T(8,128)(2,1)} %all-gather.3.cloned.1.call-done) | non-fusion elementwise | flops 1179648 | bytes 7077888 | tf_op jit(solution)/shard_map/convert_element_type | solution.py:69
  119.9 48.6 %all-gather.5.cloned.1.call-done = bf16[5,1024,320]{2,1,0:T(8,128)(2,1)} async-done(((bf16[5,64,320]{2,1,0:T(8,128)(2,1)}), bf16[5,1024,320]{2,1,0:T(8,128)(2,1)}) %all-gather.5.cloned.1.call-update) | async-done | bytes 3276816 | tf_op jit(solution)/shard_map/all_gather | solution.py:133
  168.5 10.6 %multiply_convert_fusion = bf16[5,6,192,320]{3,2,1,0:T(8,128)(2,1)S(1)} fusion(bf16[5,6,192,320]{3,2,1,0:T(8,128)(2,1)} %param.18, f32[5,192]{1,0:T(8,128)S(1)} %fusion.52, bf16[5,1024,320]{2,1,0:T(8,128)(2,1)} %all-gather.5.cloned.1.call-done, f32[5,1024]{1,0:T(8,128)S(1)} %copy-done.7, f32[5,1024]{1,0:T(8,128)S(1)} %copy-done.6, ...), kind=kOutput, calls=%fused_computation.11 | convolution fusion | flops 3799941120 | bytes 15412992 | tf_op jit(solution)/shard_map/krnd,kdo->krno/dot_general | solution.py:73
  179.2 7.2 %multiply_reduce_fusion = bf16[6,192,1024]{2,1,0:T(8,128)(2,1)S(1)} fusion(f32[5,1024]{1,0:T(8,128)S(1)} %copy-done.6, bf16[5,6,192,320]{3,2,1,0:T(8,128)(2,1)S(1)} %multiply_convert_fusion, bf16[5,1024,320]{2,1,0:T(8,128)(2,1)S(1)} %copy-done.5), kind=kOutput, calls=%fused_computation.1 | convolution fusion | flops 3785490432 | bytes 9342976 | tf_op jit(solution)/shard_map/krno,kdo->krnd/dot_general | solution.py:77
  188.2 9.3 %fusion.14 = bf16[1024,5,320]{0,2,1:T(8,128)(2,1)} fusion(bf16[5,6,192,320]{3,2,1,0:T(8,128)(2,1)} %copy-done.11, f32[5,1024]{1,0:T(8,128)S(1)} %copy-done.7, f32[5,1024]{1,0:T(8,128)S(1)} %copy-done.6, f32[6,192,1024]{2,1,0:T(8,128)} %convert_element_type.67), kind=kOutput, calls=%fused_computation.21 | convolution fusion | flops 3795845120 | bytes 11722752 | tf_op jit(solution)/shard_map/krnd,krno->dko/dot_general | solution.py:79
  197.5 8.2 %copy.54 = bf16[1024,5,320]{2,1,0:T(8,128)(2,1)} copy(bf16[1024,5,320]{0,2,1:T(8,128)(2,1)} %fusion.14) | data formatting | bytes 6553600 | tf_op jit(solution)/shard_map/convert_element_type | solution.py:151
  205.7 16.5 %reduce-scatter.7.cloned.1.call-done = bf16[24,6144]{1,0:T(8,128)(2,1)} async-done(((bf16[192,6144]{1,0:T(8,128)(2,1)}), bf16[24,6144]{1,0:T(8,128)(2,1)}) %reduce-scatter.7.cloned.1.call-update) | async-done | bytes 294928
  224.4 80.9 %reduce-scatter.5.cloned.1.call-done = bf16[64,5,320]{2,1,0:T(8,128)(2,1)} async-done(((bf16[1024,5,320]{2,1,0:T(8,128)(2,1)}), bf16[64,5,320]{2,1,0:T(8,128)(2,1)}) %reduce-scatter.5.cloned.1.call-update) | async-done | bytes 204816 | tf_op jit(solution)/shard_map/reduce_scatter | solution.py:150
  (69 shorter events, 30.7 us)
Async XLA Ops:
  7.2 76.4 %copy-start = (bf16[1024,1024]{1,0:T(8,128)(2,1)S(1)}, bf16[1024,1024]{1,0:T(8,128)(2,1)}, u32[]{:S(2)}) copy-start(bf16[1024,1024]{1,0:T(8,128)(2,1)} %param.14) | copy-start | bytes 6291460
  7.2 108.4 %all-gather.3.cloned.1.call-start = ((), (), s32[]{:S(2)}) async-start(), calls=%async_computation.2 | async-start | bytes 2654208 | tf_op jit(solution)/shard_map/all_gather | solution.py:135
  8.4 6.7 %collective-permute-start = (bf16[3,24,1024]{2,1,0:T(8,128)(2,1)S(1)}, bf16[3,24,1024]{2,1,0:T(8,128)(2,1)S(1)}, u32[]{:S(2)}, u32[]{:S(2)}) collective-permute-start(bf16[3,24,1024]{2,1,0:T(8,128)(2,1)S(1)} %get-tuple-element.25), channel_id=1, source_target_pairs={{0,8},{8,16},{16,24},{24,32},{32,40},{40,48},{48,56},{56,64},{64,7... | collective-permute-start | bytes 442376 | tf_op jit(solution)/shard_map/ppermute | solution.py:20
  12.0 7.2 %collective-permute-start.1 = (bf16[3,24,1024]{2,1,0:T(8,128)(2,1)S(1)}, bf16[3,24,1024]{2,1,0:T(8,128)(2,1)S(1)}, u32[]{:S(2)}, u32[]{:S(2)}) collective-permute-start(bf16[3,24,1024]{2,1,0:T(8,128)(2,1)S(1)} %get-tuple-element.24), channel_id=1, source_target_pairs={{8,0},{16,8},{24,16},{32,24},{40,32},{48,40},{56,48},{64,56},{72,6... | collective-permute-start | bytes 442376 | tf_op jit(solution)/shard_map/ppermute | solution.py:21
  19.2 6.3 %collective-permute-start.2 = (bf16[12,6,1024]{2,1,0:T(8,128)(2,1)S(1)}, bf16[12,6,1024]{2,1,0:T(8,128)(2,1)S(1)}, u32[]{:S(2)}, u32[]{:S(2)}) collective-permute-start(bf16[12,6,1024]{2,1,0:T(8,128)(2,1)S(1)} %get-tuple-element.22), channel_id=1, source_target_pairs={{0,1},{1,2},{2,3},{3,4},{4,5},{5,6},{6,7},{7,0},{8,9},{9,10},{10,1... | collective-permute-start | bytes 442376 | tf_op jit(solution)/shard_map/ppermute | solution.py:20
  19.3 6.3 %collective-permute-start.3 = (bf16[12,6,1024]{2,1,0:T(8,128)(2,1)S(1)}, bf16[12,6,1024]{2,1,0:T(8,128)(2,1)S(1)}, u32[]{:S(2)}, u32[]{:S(2)}) collective-permute-start(bf16[12,6,1024]{2,1,0:T(8,128)(2,1)S(1)} %get-tuple-element.23), channel_id=1, source_target_pairs={{1,0},{2,1},{3,2},{4,3},{5,4},{6,5},{7,6},{0,7},{9,8},{10,9},{11,1... | collective-permute-start | bytes 442376 | tf_op jit(solution)/shard_map/ppermute | solution.py:21
  27.9 4.5 %copy-start.4 = (f32[1024]{0:T(1024)S(1)}, f32[1024]{0:T(1024)}, u32[]{:S(2)}) copy-start(f32[1024]{0:T(1024)} %param.12) | copy-start | bytes 12292
  38.0 3.2 %copy-start.2 = (f32[432,1024]{1,0:T(8,128)S(1)}, f32[432,1024]{1,0:T(8,128)}, u32[]{:S(2)}) copy-start(f32[432,1024]{1,0:T(8,128)} %reshape.102) | copy-start | bytes 5308420
  69.5 1.8 copy-start.3
  82.5 4.2 %copy-start.8 = (s32[4]{0:T(128)S(1)}, s32[4]{0:T(128)}, u32[]{:S(2)}) copy-start(s32[4]{0:T(128)} %param.19) | copy-start | bytes 52
  82.5 4.2 %copy-start.9 = (s32[1,8]{1,0:T(1,128)S(1)}, s32[1,8]{1,0:T(1,128)}, u32[]{:S(2)}) copy-start(s32[1,8]{1,0:T(1,128)} %param.20) | copy-start | bytes 100
  82.5 4.3 %copy-start.10 = (s32[5]{0:T(128)S(1)}, s32[5]{0:T(128)}, u32[]{:S(2)}) copy-start(s32[5]{0:T(128)} %param.21) | copy-start | bytes 64
  85.9 82.6 %all-gather.5.cloned.1.call-start = ((), (), s32[]{:S(2)}) async-start(), calls=%async_computation.3 | async-start | bytes 4177920 | tf_op jit(solution)/shard_map/all_gather | solution.py:133
  86.6 135.5 %reduce-scatter.7.cloned.1.call-start = ((), (), s32[]{:S(2)}) async-start(), calls=%async_computation.5 | async-start | bytes 2654208
  87.1 81.5 %copy-start.6 = (f32[5,1024]{1,0:T(8,128)S(1)}, f32[5,1024]{1,0:T(8,128)}, u32[]{:S(2)}) copy-start(f32[5,1024]{1,0:T(8,128)} %param.15) | copy-start | bytes 61444
  87.1 81.5 %copy-start.7 = (f32[5,1024]{1,0:T(8,128)S(1)}, f32[5,1024]{1,0:T(8,128)}, u32[]{:S(2)}) copy-start(f32[5,1024]{1,0:T(8,128)} %param.16) | copy-start | bytes 61444
  168.5 10.6 %copy-start.5 = (bf16[5,1024,320]{2,1,0:T(8,128)(2,1)S(1)}, bf16[5,1024,320]{2,1,0:T(8,128)(2,1)}, u32[]{:S(2)}) copy-start(bf16[5,1024,320]{2,1,0:T(8,128)(2,1)} %all-gather.5.cloned.1.call-done) | copy-start | bytes 9830404
  179.2 7.2 %copy-start.11 = (bf16[5,6,192,320]{3,2,1,0:T(8,128)(2,1)}, bf16[5,6,192,320]{3,2,1,0:T(8,128)(2,1)S(1)}, u32[]{:S(2)}) copy-start(bf16[5,6,192,320]{3,2,1,0:T(8,128)(2,1)S(1)} %multiply_convert_fusion) | copy-start | bytes 11059204
  188.1 117.2 %reduce-scatter.5.cloned.1.call-start = ((), (), s32[]{:S(2)}) async-start(), calls=%async_computation.4 | async-start | bytes 6684672 | tf_op jit(solution)/shard_map/reduce_scatter | solution.py:150
  205.7 101.6 %copy-start.1 = (bf16[1024,1024]{1,0:T(8,128)(2,1)S(1)}, bf16[1024,1024]{1,0:T(8,128)(2,1)}, u32[]{:S(2)}) copy-start(bf16[1024,1024]{1,0:T(8,128)(2,1)} %param.14) | copy-start | bytes 6291460
Sparse Core Ops, SparseCore 0:
  86.0 29.4 all-gather.2
  117.7 50.7 all-gather.4
  188.2 33.9 reduce-scatter.6
  225.5 79.7 reduce-scatter.4
where the time goes:
time: 315 us; the launch traced here: 314 us
  waiting for transfers between devices  183 us (58%)
  local copies, waits for them, and re-layouts  53.8 us (17%)
  matrix products  42.2 us (13%)
  between operations  14 us (4%)
  other arithmetic  12.5 us (4%)
  starting transfers between devices  7.98 us (3%)
    reduce_scatter x1, waiting for transfers between devices, local(): lax.psum_scatter(head_terms.astype(jnp.bfloat16), 'lat', scatter_dimensio...  80.9 us
    all_gather x1, waiting for transfers between devices, local(): heads_full = lax.all_gather(head_weight, 'lat', axis=1, tiled=True)  48.6 us
    all_gather x1, waiting for transfers between devices, local(): piece = lax.all_gather(latent, 'var', axis=1, tiled=True)  28.5 us
    unnamed x5, waiting for transfers between devices  17.3 us
    unnamed x32, local copies, waits for them, and re-layouts  13.9 us
    dot_general x1, matrix products, slot_terms(): jnp.einsum('krnd,kdo->krno', rows, heads_full, preferred_element_type=jnp...  10.6 us
    dot_general x1, matrix products, slot_terms(): jnp.einsum('krnd,krno->dko', rows, errors, preferred_element_type=jnp.flo...  9.29 us
    another operation x2, local copies, waits for them, and re-layouts, split(): shaped = values.reshape(win_rows, WH, win_cols, WW, parts, heads, head_size)  8.98 us
  transfers between devices with their start and end apart: 8, of which 7 were waited for; matrix products, arithmetic and copies ran while one was open for 8% of the time, Pallas kernels for 0%

commit v1 on v0

--- a/solution.py
+++ b/solution.py
@@ -8,6 +8,16 @@
 WH = 6
 WW = 12
 EPS = 1e-05
+
+
+def pass_along(shard, axis, d):
+    devices = lax.axis_size(axis)
+    block, pieces = (shard, [shard])
+    for _ in range(devices - 1):
+        block = lax.ppermute(block, axis, [(i, (i + 1) % devices) for i in range(devices)])
+        pieces.insert(0, block)
+    line = jnp.concatenate(pieces, axis=d)
+    return jnp.roll(line, (lax.axis_index(axis) + 1) * shard.shape[d], axis=d)
 
 
 def padded(array, sides, width, wrap):
@@ -132,7 +142,7 @@
     live_tiles = (slot_level[None, :] < tile_levels[:, None]).astype(jnp.float32)
     heads_full = lax.all_gather(head_weight, "lat", axis=1, tiled=True)
     tile_ids = jnp.arange(var_count, dtype=jnp.int32)
-    piece = lax.all_gather(latent, "var", axis=1, tiled=True)
+    piece = pass_along(latent, "var", 1)
     piece_cols = piece.shape[1]
     column_tile = jnp.arange(piece_cols, dtype=jnp.int32) // band_cols
     onehot = (column_tile[:, None] == tile_ids[None, :]).astype(jnp.float32)

time: 315 us -> 287 us (0.911)
  waiting for transfers between devices: 183 us -> 156 us
    ppermute x0 -> x7, waiting for transfers between devices: none -> 50 us  [pass_along(): lax.ppermute(block, axis, [(i, (i + 1) % devices) for i in range(devices)])]
    all_gather x1, waiting for transfers between devices: 48.6 us -> 0.01 us  [local(): heads_full = lax.all_gather(head_weight, 'lat', axis=1, tiled=True)]
    all_gather x1 -> x0, waiting for transfers between devices: 28.5 us -> none  [local(): piece = lax.all_gather(latent, 'var', axis=1, tiled=True)]
    unnamed x32 -> x47, local copies, waits for them, and re-layouts: 13.9 us -> 14.2 us
    unnamed x5 -> x4, waiting for transfers between devices: 17.3 us -> 17.2 us
  transfers between devices with their start and end apart: 8 -> 14, of which waited for: 7 -> 12; matrix products, arithmetic and copies ran while one was open for 8% -> 30% of each run, Pallas kernels for 0% -> 0%
where the time goes in v1:
time: 287 us; the launch traced here: 286 us
  waiting for transfers between devices  156 us (54%)
  local copies, waits for them, and re-layouts  54.1 us (19%)
  matrix products  41.5 us (14%)
  between operations  14.1 us (5%)
  other arithmetic  11 us (4%)
  starting transfers between devices  9.21 us (3%)
    reduce_scatter x1, waiting for transfers between devices, local(): lax.psum_scatter(head_terms.astype(jnp.bfloat16), 'lat', scatter_dimensio...  81.1 us
    ppermute x7, waiting for transfers between devices, pass_along(): lax.ppermute(block, axis, [(i, (i + 1) % devices) for i in range(devices)])  50 us
    unnamed x4, waiting for transfers between devices  17.2 us
    unnamed x47, local copies, waits for them, and re-layouts  14.2 us
    dot_general x1, matrix products, slot_terms(): jnp.einsum('krnd,kdo->krno', rows, heads_full, preferred_element_type=jnp...  9.92 us
    dot_general x1, matrix products, slot_terms(): jnp.einsum('krnd,krno->dko', rows, errors, preferred_element_type=jnp.flo...  9.28 us
    another operation x2, local copies, waits for them, and re-layouts, split(): shaped = values.reshape(win_rows, WH, win_cols, WW, parts, heads, head_size)  8.97 us
    convert_element_type x1, local copies, waits for them, and re-layouts, local(): head_terms.astype(jnp.bfloat16)  8.2 us
  transfers between devices with their start and end apart: 14, of which 12 were waited for; matrix products, arithmetic and copies ran while one was open for 30% of the time, Pallas kernels for 0%

profile of v1, /device:TPU:0, one launch (start us, length us, event | category | flops | bytes accessed | tf_op | source)
XLA Modules:
  0.0 286.1 jit_solution(12468683539422280418)
XLA Ops:
  8.4 3.6 %collective-permute-start = (bf16[3,24,1024]{2,1,0:T(8,128)(2,1)S(1)}, bf16[3,24,1024]{2,1,0:T(8,128)(2,1)S(1)}, u32[]{:S(2)}, u32[]{:S(2)}) collective-permute-start(bf16[3,24,1024]{2,1,0:T(8,128)(2,1)S(1)} %get-tuple-element.25), channel_id=1, source_target_pairs={{0,8},{8,16},{16,24},{24,32},{32,40},{40,48},{48,56},{56,64},{64,7... | collective-permute-start | bytes 442376 | tf_op jit(solution)/shard_map/ppermute | solution.py:30
  16.0 3.1 %collective-permute-done.1 = bf16[3,24,1024]{2,1,0:T(8,128)(2,1)S(1)} collective-permute-done((bf16[3,24,1024]{2,1,0:T(8,128)(2,1)S(1)}, bf16[3,24,1024]{2,1,0:T(8,128)(2,1)S(1)}, u32[]{:S(2)}, u32[]{:S(2)}) %collective-permute-start.1) | collective-permute-done | bytes 147488 | tf_op jit(solution)/shard_map/ppermute | solution.py:31
  22.5 3.1 %collective-permute-done.2 = bf16[12,6,1024]{2,1,0:T(8,128)(2,1)S(1)} collective-permute-done((bf16[12,6,1024]{2,1,0:T(8,128)(2,1)S(1)}, bf16[12,6,1024]{2,1,0:T(8,128)(2,1)S(1)}, u32[]{:S(2)}, u32[]{:S(2)}) %collective-permute-start.2) | collective-permute-done | bytes 147488 | tf_op jit(solution)/shard_map/ppermute | solution.py:30
  38.1 3.1 %copy.48 = bf16[2,3,6,12,1,16,64]{6,5,3,2,1,0,4:T(8,128)(2,1)} copy(bf16[2,3,6,12,1,16,64]{6,5,3,1,2,0,4:T(8,128)(2,1)} %bitcast.58) | data formatting | bytes 1769472 | tf_op jit(solution)/shard_map/transpose | solution.py:52
  41.2 6.1 %fusion.15 = bf16[432,2048]{1,0:T(8,128)(2,1)} fusion(bf16[1024,3072]{1,0:T(8,128)(2,1)} %param.13, f32[432,1024]{1,0:T(8,128)} %reshape.102, f32[1024]{0:T(1024)S(1)} %copy-done.4, f32[432]{0:T(512)S(1)} %rsqrt.13, f32[432]{0:T(512)S(1)} %div.33), kind=kOutput, calls=%fused_computation.22 | convolution fusion | flops 1814593536 | bytes 7740800 | tf_op jit(solution)/shard_map/dot_general | solution.py:117
  47.3 6.4 %reshape_reshape.3 = bf16[2,6,3,12,2,16,64]{6,5,4,3,2,1,0:T(8,128)(2,1)} reshape(bf16[432,2048]{1,0:T(8,128)(2,1)} %fusion.15) | data formatting | bytes 3538944 | tf_op jit(solution)/shard_map/reshape;reshape | solution.py:51
  58.8 4.0 %copy.61 = bf16[6,72,1,16,64]{1,4,3,0,2:T(8,128)(2,1)} copy(bf16[6,72,1,16,64]{4,3,2,1,0:T(8,128)(2,1)} %get-tuple-element.18) | data formatting | bytes 1769472
  62.9 4.1 %copy.62 = bf16[6,72,1,16,64]{1,4,3,0,2:T(8,128)(2,1)} copy(bf16[6,72,1,16,64]{4,3,2,1,0:T(8,128)(2,1)} %get-tuple-element.19) | data formatting | bytes 1769472
  66.9 3.1 %fusion.25 = f32[6,16,72,72]{2,3,1,0:T(8,128)S(1)} fusion(bf16[6,72,16,64]{3,2,1,0:T(8,128)(2,1)} %bitcast.59, bf16[6,72,1,16,64]{1,4,3,0,2:T(8,128)(2,1)} %copy.62), kind=kOutput, calls=%fused_computation.30 | convolution fusion | flops 63700992 | bytes 3760128 | tf_op jit(solution)/shard_map/wqhd,wkhd->whqk/dot_general | solution.py:63
  73.8 4.0 %copy.52 = bf16[6,72,16,64]{3,2,1,0:T(8,128)(2,1)} copy(bf16[6,72,16,64]{1,3,2,0:T(8,128)(2,1)} %fusion.34) | data formatting | bytes 1769472 | tf_op jit(solution)/shard_map/whqk,wkhd->wqhd/transpose | solution.py:70
  77.8 3.9 %reshape.100 = bf16[2,3,6,12,1024]{4,3,2,1,0:T(8,128)(2,1)} reshape(bf16[6,72,16,64]{3,2,1,0:T(8,128)(2,1)} %copy.52) | data formatting | bytes 1769472 | tf_op jit(solution)/shard_map/reshape | solution.py:72
  87.1 6.2 %collective-permute-done.4 = bf16[6,24,1024]{2,1,0:T(8,128)(2,1)S(1)} collective-permute-done((bf16[6,24,1024]{2,1,0:T(8,128)(2,1)S(1)}, bf16[6,24,1024]{2,1,0:T(8,128)(2,1)S(1)}, u32[]{:S(2)}, u32[]{:S(2)}) %collective-permute-start.4) | collective-permute-done | bytes 294944 | tf_op jit(solution)/shard_map/ppermute | solution.py:17
  93.3 7.4 %collective-permute-done.5 = bf16[6,24,1024]{2,1,0:T(8,128)(2,1)S(1)} collective-permute-done((bf16[6,24,1024]{2,1,0:T(8,128)(2,1)S(1)}, bf16[6,24,1024]{2,1,0:T(8,128)(2,1)S(1)}, u32[]{:S(2)}, u32[]{:S(2)}) %collective-permute-start.5) | collective-permute-done | bytes 294944 | tf_op jit(solution)/shard_map/ppermute | solution.py:17
  100.6 7.4 %collective-permute-done.6 = bf16[6,24,1024]{2,1,0:T(8,128)(2,1)S(1)} collective-permute-done((bf16[6,24,1024]{2,1,0:T(8,128)(2,1)S(1)}, bf16[6,24,1024]{2,1,0:T(8,128)(2,1)S(1)}, u32[]{:S(2)}, u32[]{:S(2)}) %collective-permute-start.6) | collective-permute-done | bytes 294944 | tf_op jit(solution)/shard_map/ppermute | solution.py:17
  108.0 7.4 %collective-permute-done.7 = bf16[6,24,1024]{2,1,0:T(8,128)(2,1)S(1)} collective-permute-done((bf16[6,24,1024]{2,1,0:T(8,128)(2,1)S(1)}, bf16[6,24,1024]{2,1,0:T(8,128)(2,1)S(1)}, u32[]{:S(2)}, u32[]{:S(2)}) %collective-permute-start.7) | collective-permute-done | bytes 294944 | tf_op jit(solution)/shard_map/ppermute | solution.py:17
  115.4 7.4 %collective-permute-done.8 = bf16[6,24,1024]{2,1,0:T(8,128)(2,1)S(1)} collective-permute-done((bf16[6,24,1024]{2,1,0:T(8,128)(2,1)S(1)}, bf16[6,24,1024]{2,1,0:T(8,128)(2,1)S(1)}, u32[]{:S(2)}, u32[]{:S(2)}) %collective-permute-start.8) | collective-permute-done | bytes 294944 | tf_op jit(solution)/shard_map/ppermute | solution.py:17
  122.8 7.3 %collective-permute-done.9 = bf16[6,24,1024]{2,1,0:T(8,128)(2,1)S(1)} collective-permute-done((bf16[6,24,1024]{2,1,0:T(8,128)(2,1)S(1)}, bf16[6,24,1024]{2,1,0:T(8,128)(2,1)S(1)}, u32[]{:S(2)}, u32[]{:S(2)}) %collective-permute-start.9) | collective-permute-done | bytes 294944 | tf_op jit(solution)/shard_map/ppermute | solution.py:17
  130.3 7.1 %collective-permute-done.10 = bf16[6,24,1024]{2,1,0:T(8,128)(2,1)S(1)} collective-permute-done((bf16[6,24,1024]{2,1,0:T(8,128)(2,1)S(1)}, bf16[6,24,1024]{2,1,0:T(8,128)(2,1)S(1)}, u32[]{:S(2)}, u32[]{:S(2)}) %collective-permute-start.10) | collective-permute-done | bytes 294944 | tf_op jit(solution)/shard_map/ppermute | solution.py:17
  140.8 9.9 %multiply_convert_fusion = bf16[5,6,192,320]{3,2,1,0:T(8,128)(2,1)S(1)} fusion(bf16[5,6,192,320]{3,2,1,0:T(8,128)(2,1)} %param.18, f32[5,192]{1,0:T(8,128)S(1)} %fusion.52, bf16[5,1024,320]{2,1,0:T(8,128)(2,1)} %all-gather.2.cloned.1.call-done, f32[5,1024]{1,0:T(8,128)S(1)} %copy-done.7, f32[5,1024]{1,0:T(8,128)S(1)} %copy-done.6, ...), kind=kOutput, calls=%fused_computation.11 | convolution fusion | flops 3799941120 | bytes 15412992 | tf_op jit(solution)/shard_map/krnd,kdo->krno/dot_general | solution.py:83
  150.7 7.2 %multiply_reduce_fusion = bf16[6,192,1024]{2,1,0:T(8,128)(2,1)S(1)} fusion(f32[5,1024]{1,0:T(8,128)S(1)} %copy-done.6, bf16[5,6,192,320]{3,2,1,0:T(8,128)(2,1)S(1)} %multiply_convert_fusion, bf16[5,1024,320]{2,1,0:T(8,128)(2,1)S(1)} %copy-done.5), kind=kOutput, calls=%fused_computation.1 | convolution fusion | flops 3785490432 | bytes 9342976 | tf_op jit(solution)/shard_map/krno,kdo->krnd/dot_general | solution.py:87
  159.7 9.3 %fusion.14 = bf16[1024,5,320]{0,2,1:T(8,128)(2,1)} fusion(bf16[5,6,192,320]{3,2,1,0:T(8,128)(2,1)} %copy-done.11, f32[5,1024]{1,0:T(8,128)S(1)} %copy-done.7, f32[5,1024]{1,0:T(8,128)S(1)} %copy-done.6, f32[6,192,1024]{2,1,0:T(8,128)} %dynamic-slice_convert_fusion), kind=kOutput, calls=%fused_computation.21 | convolution fusion | flops 3795845120 | bytes 11722752 | tf_op jit(solution)/shard_map/krnd,krno->dko/dot_general | solution.py:89
  169.0 8.2 %copy.54 = bf16[1024,5,320]{2,1,0:T(8,128)(2,1)} copy(bf16[1024,5,320]{0,2,1:T(8,128)(2,1)} %fusion.14) | data formatting | bytes 6553600 | tf_op jit(solution)/shard_map/convert_element_type | solution.py:161
  177.2 17.1 %reduce-scatter.7.cloned.1.call-done = bf16[24,6144]{1,0:T(8,128)(2,1)} async-done(((bf16[192,6144]{1,0:T(8,128)(2,1)}), bf16[24,6144]{1,0:T(8,128)(2,1)}) %reduce-scatter.7.cloned.1.call-update) | async-done | bytes 294928
  196.6 81.1 %reduce-scatter.5.cloned.1.call-done = bf16[64,5,320]{2,1,0:T(8,128)(2,1)} async-done(((bf16[1024,5,320]{2,1,0:T(8,128)(2,1)}), bf16[64,5,320]{2,1,0:T(8,128)(2,1)}) %reduce-scatter.5.cloned.1.call-update) | async-done | bytes 204816 | tf_op jit(solution)/shard_map/reduce_scatter | solution.py:160
  (96 shorter events, 44.6 us)
Async XLA Ops:
  7.2 77.0 %copy-start = (bf16[1024,1024]{1,0:T(8,128)(2,1)S(1)}, bf16[1024,1024]{1,0:T(8,128)(2,1)}, u32[]{:S(2)}) copy-start(bf16[1024,1024]{1,0:T(8,128)(2,1)} %param.14) | copy-start | bytes 6291460
  7.2 133.6 %all-gather.2.cloned.1.call-start = ((), (), s32[]{:S(2)}) async-start(), calls=%async_computation.2 | async-start | bytes 4177920 | tf_op jit(solution)/shard_map/all_gather | solution.py:143
  8.4 6.7 %collective-permute-start = (bf16[3,24,1024]{2,1,0:T(8,128)(2,1)S(1)}, bf16[3,24,1024]{2,1,0:T(8,128)(2,1)S(1)}, u32[]{:S(2)}, u32[]{:S(2)}) collective-permute-start(bf16[3,24,1024]{2,1,0:T(8,128)(2,1)S(1)} %get-tuple-element.25), channel_id=1, source_target_pairs={{0,8},{8,16},{16,24},{24,32},{32,40},{40,48},{48,56},{56,64},{64,7... | collective-permute-start | bytes 442376 | tf_op jit(solution)/shard_map/ppermute | solution.py:30
  12.0 7.2 %collective-permute-start.1 = (bf16[3,24,1024]{2,1,0:T(8,128)(2,1)S(1)}, bf16[3,24,1024]{2,1,0:T(8,128)(2,1)S(1)}, u32[]{:S(2)}, u32[]{:S(2)}) collective-permute-start(bf16[3,24,1024]{2,1,0:T(8,128)(2,1)S(1)} %get-tuple-element.24), channel_id=1, source_target_pairs={{8,0},{16,8},{24,16},{32,24},{40,32},{48,40},{56,48},{64,56},{72,6... | collective-permute-start | bytes 442376 | tf_op jit(solution)/shard_map/ppermute | solution.py:31
  19.2 6.3 %collective-permute-start.2 = (bf16[12,6,1024]{2,1,0:T(8,128)(2,1)S(1)}, bf16[12,6,1024]{2,1,0:T(8,128)(2,1)S(1)}, u32[]{:S(2)}, u32[]{:S(2)}) collective-permute-start(bf16[12,6,1024]{2,1,0:T(8,128)(2,1)S(1)} %get-tuple-element.22), channel_id=1, source_target_pairs={{0,1},{1,2},{2,3},{3,4},{4,5},{5,6},{6,7},{7,0},{8,9},{9,10},{10,1... | collective-permute-start | bytes 442376 | tf_op jit(solution)/shard_map/ppermute | solution.py:30
  19.3 6.3 %collective-permute-start.3 = (bf16[12,6,1024]{2,1,0:T(8,128)(2,1)S(1)}, bf16[12,6,1024]{2,1,0:T(8,128)(2,1)S(1)}, u32[]{:S(2)}, u32[]{:S(2)}) collective-permute-start(bf16[12,6,1024]{2,1,0:T(8,128)(2,1)S(1)} %get-tuple-element.23), channel_id=1, source_target_pairs={{1,0},{2,1},{3,2},{4,3},{5,4},{6,5},{7,6},{0,7},{9,8},{10,9},{11,1... | collective-permute-start | bytes 442376 | tf_op jit(solution)/shard_map/ppermute | solution.py:31
  22.2 172.1 %reduce-scatter.7.cloned.1.call-start = ((), (), s32[]{:S(2)}) async-start(), calls=%async_computation.4 | async-start | bytes 2654208
  27.9 4.4 %copy-start.4 = (f32[1024]{0:T(1024)S(1)}, f32[1024]{0:T(1024)}, u32[]{:S(2)}) copy-start(f32[1024]{0:T(1024)} %param.12) | copy-start | bytes 12292
  81.7 41.0 %copy-start.8 = (s32[4]{0:T(128)S(1)}, s32[4]{0:T(128)}, u32[]{:S(2)}) copy-start(s32[4]{0:T(128)} %param.19) | copy-start | bytes 52
  81.7 41.0 %copy-start.9 = (s32[1,8]{1,0:T(1,128)S(1)}, s32[1,8]{1,0:T(1,128)}, u32[]{:S(2)}) copy-start(s32[1,8]{1,0:T(1,128)} %param.20) | copy-start | bytes 100
  81.7 48.3 %copy-start.10 = (s32[5]{0:T(128)S(1)}, s32[5]{0:T(128)}, u32[]{:S(2)}) copy-start(s32[5]{0:T(128)} %param.21) | copy-start | bytes 64
  85.8 52.1 %copy-start.3 = (bf16[6,24,1024]{2,1,0:T(8,128)(2,1)}, bf16[6,24,1024]{2,1,0:T(8,128)(2,1)S(1)}, u32[]{:S(2)}) copy-start(bf16[6,24,1024]{2,1,0:T(8,128)(2,1)S(1)} %fusion.43) | copy-start | bytes 884740
  85.8 7.5 %collective-permute-start.4 = (bf16[6,24,1024]{2,1,0:T(8,128)(2,1)S(1)}, bf16[6,24,1024]{2,1,0:T(8,128)(2,1)S(1)}, u32[]{:S(2)}, u32[]{:S(2)}) collective-permute-start(bf16[6,24,1024]{2,1,0:T(8,128)(2,1)S(1)} %fusion.43), channel_id=1, source_target_pairs={{0,1},{1,2},{2,3},{3,4},{4,5},{5,6},{6,7},{7,0},{8,9},{9,10},{10,1... | collective-permute-start | bytes 884744 | tf_op jit(solution)/shard_map/ppermute | solution.py:17
  93.3 7.4 %collective-permute-start.5 = (bf16[6,24,1024]{2,1,0:T(8,128)(2,1)S(1)}, bf16[6,24,1024]{2,1,0:T(8,128)(2,1)S(1)}, u32[]{:S(2)}, u32[]{:S(2)}) collective-permute-start(bf16[6,24,1024]{2,1,0:T(8,128)(2,1)S(1)} %collective-permute-done.4), channel_id=1, source_target_pairs={{0,1},{1,2},{2,3},{3,4},{4,5},{5,6},{6,7},{7,0},{8,9},{9,10},{10,1... | collective-permute-start | bytes 884744 | tf_op jit(solution)/shard_map/ppermute | solution.py:17
  100.6 7.4 %collective-permute-start.6 = (bf16[6,24,1024]{2,1,0:T(8,128)(2,1)S(1)}, bf16[6,24,1024]{2,1,0:T(8,128)(2,1)S(1)}, u32[]{:S(2)}, u32[]{:S(2)}) collective-permute-start(bf16[6,24,1024]{2,1,0:T(8,128)(2,1)S(1)} %collective-permute-done.5), channel_id=1, source_target_pairs={{0,1},{1,2},{2,3},{3,4},{4,5},{5,6},{6,7},{7,0},{8,9},{9,10},{10,1... | collective-permute-start | bytes 884744 | tf_op jit(solution)/shard_map/ppermute | solution.py:17
  108.0 7.4 %collective-permute-start.7 = (bf16[6,24,1024]{2,1,0:T(8,128)(2,1)S(1)}, bf16[6,24,1024]{2,1,0:T(8,128)(2,1)S(1)}, u32[]{:S(2)}, u32[]{:S(2)}) collective-permute-start(bf16[6,24,1024]{2,1,0:T(8,128)(2,1)S(1)} %collective-permute-done.6), channel_id=1, source_target_pairs={{0,1},{1,2},{2,3},{3,4},{4,5},{5,6},{6,7},{7,0},{8,9},{9,10},{10,1... | collective-permute-start | bytes 884744 | tf_op jit(solution)/shard_map/ppermute | solution.py:17
  115.4 7.4 %collective-permute-start.8 = (bf16[6,24,1024]{2,1,0:T(8,128)(2,1)S(1)}, bf16[6,24,1024]{2,1,0:T(8,128)(2,1)S(1)}, u32[]{:S(2)}, u32[]{:S(2)}) collective-permute-start(bf16[6,24,1024]{2,1,0:T(8,128)(2,1)S(1)} %collective-permute-done.7), channel_id=1, source_target_pairs={{0,1},{1,2},{2,3},{3,4},{4,5},{5,6},{6,7},{7,0},{8,9},{9,10},{10,1... | collective-permute-start | bytes 884744 | tf_op jit(solution)/shard_map/ppermute | solution.py:17
  122.7 7.4 %collective-permute-start.9 = (bf16[6,24,1024]{2,1,0:T(8,128)(2,1)S(1)}, bf16[6,24,1024]{2,1,0:T(8,128)(2,1)S(1)}, u32[]{:S(2)}, u32[]{:S(2)}) collective-permute-start(bf16[6,24,1024]{2,1,0:T(8,128)(2,1)S(1)} %collective-permute-done.8), channel_id=1, source_target_pairs={{0,1},{1,2},{2,3},{3,4},{4,5},{5,6},{6,7},{7,0},{8,9},{9,10},{10,1... | collective-permute-start | bytes 884744 | tf_op jit(solution)/shard_map/ppermute | solution.py:17
  130.1 7.4 %collective-permute-start.10 = (bf16[6,24,1024]{2,1,0:T(8,128)(2,1)S(1)}, bf16[6,24,1024]{2,1,0:T(8,128)(2,1)S(1)}, u32[]{:S(2)}, u32[]{:S(2)}) collective-permute-start(bf16[6,24,1024]{2,1,0:T(8,128)(2,1)S(1)} %collective-permute-done.9), channel_id=1, source_target_pairs={{0,1},{1,2},{2,3},{3,4},{4,5},{5,6},{6,7},{7,0},{8,9},{9,10},{10,1... | collective-permute-start | bytes 884744 | tf_op jit(solution)/shard_map/ppermute | solution.py:17
  137.9 2.9 %copy-start.6 = (f32[5,1024]{1,0:T(8,128)S(1)}, f32[5,1024]{1,0:T(8,128)}, u32[]{:S(2)}) copy-start(f32[5,1024]{1,0:T(8,128)} %param.15) | copy-start | bytes 61444
  140.8 9.9 %copy-start.5 = (bf16[5,1024,320]{2,1,0:T(8,128)(2,1)S(1)}, bf16[5,1024,320]{2,1,0:T(8,128)(2,1)}, u32[]{:S(2)}) copy-start(bf16[5,1024,320]{2,1,0:T(8,128)(2,1)} %all-gather.2.cloned.1.call-done) | copy-start | bytes 9830404
  150.7 7.2 %copy-start.11 = (bf16[5,6,192,320]{3,2,1,0:T(8,128)(2,1)}, bf16[5,6,192,320]{3,2,1,0:T(8,128)(2,1)S(1)}, u32[]{:S(2)}) copy-start(bf16[5,6,192,320]{3,2,1,0:T(8,128)(2,1)S(1)} %multiply_convert_fusion) | copy-start | bytes 11059204
  159.7 118.0 %reduce-scatter.5.cloned.1.call-start = ((), (), s32[]{:S(2)}) async-start(), calls=%async_computation.3 | async-start | bytes 6684672 | tf_op jit(solution)/shard_map/reduce_scatter | solution.py:160
  177.2 102.4 %copy-start.1 = (bf16[1024,1024]{1,0:T(8,128)(2,1)S(1)}, bf16[1024,1024]{1,0:T(8,128)(2,1)}, u32[]{:S(2)}) copy-start(bf16[1024,1024]{1,0:T(8,128)(2,1)} %param.14) | copy-start | bytes 6291460
  (2 other events, 4.7 us)
Sparse Core Ops, SparseCore 0:
  22.3 52.7 all-gather.1
  159.8 34.4 reduce-scatter.6
  197.8 79.8 reduce-scatter.4
